TPU v7x, 32 devices: a whole 2x2x4 slice. The times are simulated.
32 devices in a mesh: dp: 4 (over y, x), px: 4 (over z), py: 2 (over core).
Axes of the slice: x: 2, y: 2, z: 4, core: 2. Of those that a mesh axis runs over, the one named last changes fastest.
Arguments:
- fields: bfloat16 [4, 16, 16, 32, 256], P('dp', 'px', 'py'), may hold values from -6 to 6
- cotangent: bfloat16 [4, 16, 16, 32, 256], P('dp', 'px', 'py'), may hold values from -6 to 6
- first_weight: bfloat16 [6912, 256], replicated, may hold values from -0.078125 to 0.078125
- second_weight: bfloat16 [6912, 256], replicated, may hold values from -0.078125 to 0.078125
Outputs:
- output: bfloat16 [4, 16, 16, 32, 256], P('dp', 'px', 'py')
- field_grad: bfloat16 [4, 16, 16, 32, 256], P('dp', 'px', 'py')
- first_grad: float32 [6912, 256], P('dp', ('px', 'py'))
- second_grad: float32 [6912, 256], P('dp', ('px', 'py'))
All inputs are finite; a program needn't handle non-finite values.
Results may differ from a plain program's by a relative error of at most 0.0033.
Values may be sent and summed in bfloat16 or wider, within the bound.
A program may use at most 128 MiB of HBM per device.

v0:
```python
import functools

import jax
import jax.numpy as jnp
from jax import lax
from jax.experimental import pallas as pl
from jax.experimental.pallas import tpu as pltpu
from jax.sharding import PartitionSpec as P

MESH = pl.DeviceIdType.MESH
F32, BF16 = jnp.float32, jnp.bfloat16
DIRS = [(dx, dy) for dx in (-1, 0, 1) for dy in (-1, 0, 1) if dx or dy]
GELU_C = 0.7978845608028654
GELU_A = 0.044715


def gelu_parts(v):
    return jnp.tanh(GELU_C * (v + GELU_A * (v * v * v)))


def dp_slots(ndp):
    db = 2 if ndp % 2 == 0 else 1
    da = ndp // db
    first = [(0, 0, hop, item) for hop in range(1, db) for item in [*range(1, da), 0]]
    other = [(0, 1, hop, item) for hop in range(1, da) for item in [*range(1, db), 0]]
    slots = [s for pair in zip(first, other) for s in pair]
    slots += first[len(other) :] + other[len(first) :]
    slots += [(1, 0, hop, 0) for hop in range(1, da)] + [(1, 1, hop, 0) for hop in range(1, db)]
    return (da, db), slots


def results(rows, out_in, fgrad_in, g1_in, g2_in, out_ref, fgrad_ref, g1_ref, g2_ref):
    out_ref[...] = out_in[...]
    fgrad_ref[...] = fgrad_in[...]
    g1_ref[...] = g1_in[:, :rows]
    g2_ref[...] = g2_in[:, :rows]


def kernel(
    sizes,
    fields, cot, w1_hbm, w2_hbm,
    out_ref, fgrad_ref, g1_ref, g2_ref,
    w1, w2, p_f, p_c, p_h, p_g, z_a, z_b, z_c, lhs_f, lhs_h, pre,
    own, send_a, recv_a, recv_b, tot, send_z, recv_z,
    sem_w, halo_send, halo_recv, a_send, a_recv, b_send, b_recv, z_send, z_recv,
):
    ndp, npx, npy, rollouts = sizes
    factors, b_slots = dp_slots(ndp)
    nx, ny, nz, ch = fields.shape
    cells = nx * ny * nz
    half = ch // npy
    rows = own.shape[1] // ndp
    rpad = tot.shape[0]
    wid = recv_z.shape[2]
    nj = half // wid
    d, x, y = lax.axis_index("dp"), lax.axis_index("px"), lax.axis_index("py")

    load_w = [
        pltpu.make_async_copy(w1_hbm, w1, sem_w.at[0]),
        pltpu.make_async_copy(w2_hbm, w2, sem_w.at[1]),
    ]
    for copy in load_w:
        copy.start()

    barrier = pltpu.get_barrier_semaphore()
    for i in range(1, ndp):
        pl.semaphore_signal(
            barrier, inc=1, device_id=(lax.rem(d + i, ndp), x, y), device_id_type=MESH
        )
    for i in range(1, npx * npy):
        other = lax.rem(x * npy + y + i, npx * npy)
        pl.semaphore_signal(
            barrier, inc=1, device_id=(d, other // npy, lax.rem(other, npy)), device_id_type=MESH
        )
    pl.semaphore_wait(barrier, ndp - 1 + npx * npy - 1)

    def exists(dx, dy):
        return (x + dx >= 0) & (x + dx < npx) & (y + dy >= 0) & (y + dy < npy)

    def span_src(step, size, base):
        if step == 0:
            return pl.ds(base, size)
        return pl.ds(base if step < 0 else base + size - 1, 1)

    def span_dst(step, size):
        if step == 0:
            return pl.ds(1, size)
        return pl.ds(size + 1 if step < 0 else 0, 1)

    def halo_copy(which, src, base, padded, index):
        dx, dy = DIRS[index]
        return pltpu.make_async_remote_copy(
            src_ref=src.at[span_src(dx, nx, base), span_src(dy, ny, base)],
            dst_ref=padded.at[span_dst(dx, nx), span_dst(dy, ny)],
            send_sem=halo_send.at[which, index],
            recv_sem=halo_recv.at[which, index],
            device_id=(d, x + dx, y + dy),
            device_id_type=MESH,
        )

    def halo_start(which, src, base, padded):
        for index, (dx, dy) in enumerate(DIRS):
            @pl.when(exists(dx, dy))
            def _():
                halo_copy(which, src, base, padded, index).start()

            @pl.when(jnp.logical_not(exists(-dx, -dy)))
            def _():
                sx, sy = span_dst(dx, nx), span_dst(dy, ny)
                padded[sx, sy] = jnp.zeros((sx.size, sy.size, nz, ch), BF16)

    def halo_wait(which, src, base, padded):
        for index, (dx, dy) in enumerate(DIRS):
            @pl.when(exists(dx, dy))
            def _():
                halo_copy(which, src, base, padded, index).wait_send()

            @pl.when(exists(-dx, -dy))
            def _():
                halo_copy(which, src, base, padded, index).wait_recv()

    def build(padded, shifted):
        @pl.loop(0, nx + 2)
        def _(i):
            plane = padded[i]
            flat = plane.reshape((ny + 2) * nz, ch).astype(F32)
            place = lax.broadcasted_iota(jnp.int32, flat.shape, 0) % nz
            low = jnp.where(place == 0, 0.0, pltpu.roll(flat, 1, 0))
            high = jnp.where(place == nz - 1, 0.0, pltpu.roll(flat, flat.shape[0] - 1, 0))
            shifted[i, :, :, 0:ch] = low.astype(BF16).reshape(plane.shape)
            shifted[i, :, :, ch : 2 * ch] = plane
            shifted[i, :, :, 2 * ch : 3 * ch] = high.astype(BF16).reshape(plane.shape)

    tile = ny * nz

    def conv(shifted, weight, flipped, finish, low=0, high=nx):
        @pl.loop(low, high)
        def _(i):
            total = None
            for a in range(3):
                for b in range(3):
                    first = (9 * a + 3 * b) * ch
                    if not flipped:
                        lhs = shifted[i + a, pl.ds(b, ny)].reshape(tile, 3 * ch)
                        term = jnp.dot(
                            lhs, weight[pl.ds(first, 3 * ch)], preferred_element_type=F32
                        )
                        total = term if total is None else total + term
                        continue
                    for c in range(3):
                        lhs = shifted[
                            i + 2 - a, pl.ds(2 - b, ny), :, pl.ds((2 - c) * ch, ch)
                        ].reshape(tile, ch)
                        term = lax.dot_general(
                            lhs,
                            weight[pl.ds(first + c * ch, ch)],
                            (((1,), (1,)), ((), ())),
                            preferred_element_type=F32,
                        )
                        total = term if total is None else total + term
            finish(i, total)

    partner = 1 - y

    def a_copy(which, step):
        part = pl.ds(pl.multiple_of(step * 3 * ch, 3 * ch), 3 * ch)
        return pltpu.make_async_remote_copy(
            src_ref=send_a.at[which, part],
            dst_ref=recv_a.at[which, part],
            send_sem=a_send.at[which, step],
            recv_sem=a_recv.at[which, step],
            device_id=(d, x, partner),
            device_id_type=MESH,
        )

    def weight_grad(which, lhs, shifted):
        @pl.loop(0, 9)
        def _(step):
            a, b = step // 3, step % 3
            rhs = shifted[pl.ds(2 - a, nx), pl.ds(2 - b, ny)].reshape(cells, 3 * ch)
            prod = jnp.dot(lhs[...], rhs, preferred_element_type=F32)
            for c in range(3):
                block = prod[:, (2 - c) * ch : (3 - c) * ch]
                here = pl.ds(pl.multiple_of(step * 3 * ch, ch) + c * ch, ch)
                low, high = block[:, :half], block[:, half:]
                own[which, here] = jnp.where(y == 0, low, high)
                send_a[which, here] = jnp.where(y == 0, high, low).astype(BF16)
            a_copy(which, step).start()

    da, db = factors
    part_rows = rows // 2
    ia, ib = d // db, lax.rem(d, db)

    def piece(a, b, side):
        first = (a * db + b) * rows + side * part_rows
        return pl.ds(pl.multiple_of(first, 16), part_rows)

    def ring(index, hop, count):
        return lax.rem(index + hop, count)

    def b_copy(which, phase, side, hop, item):
        along_b = (side == 0) == (phase == 0)
        if along_b:
            a, b = (ring(ia, item, da) if phase == 0 else ia), ring(ib, hop, db)
            peer = ia * db + b
        else:
            a, b = ring(ia, hop, da), (ring(ib, item, db) if phase == 0 else ib)
            peer = a * db + ib
        slot = b_slots.index((phase, side, hop, item))
        return piece(a, b, side), pltpu.make_async_remote_copy(
            src_ref=send_a.at[which, piece(a, b, side)],
            dst_ref=recv_b.at[which, slot],
            send_sem=b_send.at[which, slot],
            recv_sem=b_recv.at[which, slot],
            device_id=(peer, x, y),
            device_id_type=MESH,
        )

    def rows_start(which):
        @pl.loop(0, 9)
        def _(step):
            a_copy(which, step).wait()

        for slot in [s for s in b_slots if s[0] == 0]:
            part, copy = b_copy(which, *slot)
            send_a[which, part] = (own[which, part] + recv_a[which, part].astype(F32)).astype(BF16)
            copy.start()
        for side, count in ((0, da), (1, db)):
            for item in range(count):
                a, b = (ring(ia, item, da), ib) if side == 0 else (ia, ring(ib, item, db))
                part = piece(a, b, side)
                own[which, part] = own[which, part] + recv_a[which, part].astype(F32)

    def rows_next(which):
        for side, count, hops in ((0, da, db), (1, db, da)):
            for item in [*range(1, count), 0]:
                a, b = (ring(ia, item, da), ib) if side == 0 else (ia, ring(ib, item, db))
                part = piece(a, b, side)
                total = own[which, part]
                for hop in range(1, hops):
                    slot = (0, side, hop, item)
                    b_copy(which, *slot)[1].wait()
                    total = total + recv_b[which, b_slots.index(slot)].astype(F32)
                if item:
                    send_a[which, part] = total.astype(BF16)
                    b_copy(which, 1, side, item, 0)[1].start()
                else:
                    own[which, part] = total

    def z_ids(j):
        owner = y * nj + j
        return owner // npy, lax.rem(owner, npy)

    def z_remote(which, j):
        px_o, py_o = z_ids(j)
        return pltpu.make_async_remote_copy(
            src_ref=send_z.at[which, pl.ds(j * wid, wid)],
            dst_ref=recv_z.at[which, x],
            send_sem=z_send.at[which, j],
            recv_sem=z_recv.at[which, x],
            device_id=(d, px_o, py_o),
            device_id_type=MESH,
        )

    def columns_start(which):
        for side, hops in ((0, da), (1, db)):
            total = own[which, piece(ia, ib, side)]
            for hop in range(1, hops):
                slot = (1, side, hop, 0)
                b_copy(which, *slot)[1].wait()
                total = total + recv_b[which, b_slots.index(slot)].astype(F32)
            tot[side * part_rows : (side + 1) * part_rows] = total
        if rpad > rows:
            tot[rows:rpad] = jnp.zeros((rpad - rows, half), F32)
        send_z[which] = tot[...].T.astype(BF16)
        for j in range(nj):
            px_o, py_o = z_ids(j)
            mine = (px_o == x) & (py_o == y)

            @pl.when(jnp.logical_not(mine))
            def _():
                z_remote(which, j).start()

            @pl.when(mine)
            def _():
                pltpu.make_async_copy(
                    send_z.at[which, pl.ds(j * wid, wid)], recv_z.at[which, x], z_recv.at[which, x]
                ).start()

    def finish_grad(which, grad):
        for j in range(nj):
            px_o, py_o = z_ids(j)

            @pl.when(jnp.logical_not((px_o == x) & (py_o == y)))
            def _():
                z_remote(which, j).wait_send()

        total = None
        for i in range(npx):
            pltpu.make_async_copy(
                recv_z.at[which, i], recv_z.at[which, i], z_recv.at[which, i]
            ).wait()
            term = recv_z[which, i].astype(F32)
            total = term if total is None else total + term
        grad[...] = total / rollouts

    halo_start(0, fields, 0, p_f)
    halo_start(1, cot, 0, p_c)
    p_f[pl.ds(1, nx), pl.ds(1, ny)] = fields[...]
    p_c[pl.ds(1, nx), pl.ds(1, ny)] = cot[...]
    lhs_f[...] = fields[...].reshape(cells, ch).T
    halo_wait(0, fields, 0, p_f)
    build(p_f, z_a)
    load_w[0].wait()

    def hidden_finish(i, total):
        pre[i] = total
        value = (total * (0.5 * (1.0 + gelu_parts(total)))).astype(BF16)
        p_h[i + 1, pl.ds(1, ny)] = value.reshape(ny, nz, ch)

    conv(z_a, w1, False, hidden_finish)
    halo_start(2, p_h, 1, p_h)
    lhs_h[...] = p_h[pl.ds(1, nx), pl.ds(1, ny)].reshape(cells, ch).T
    halo_wait(1, cot, 0, p_c)
    build(p_c, z_b)
    weight_grad(1, lhs_h, z_b)
    rows_start(1)
    load_w[1].wait()

    def grad_finish(i, total):
        v = pre[i]
        t = gelu_parts(v)
        slope = 0.5 * (1.0 + t) + (0.5 * v) * (1.0 - t * t) * (
            GELU_C * (1.0 + (3.0 * GELU_A) * (v * v))
        )
        p_g[i + 1, pl.ds(1, ny)] = (total * slope).astype(BF16).reshape(ny, nz, ch)

    conv(z_b, w2, True, grad_finish)
    halo_start(3, p_g, 1, p_g)
    halo_wait(2, p_h, 1, p_h)
    build(p_h, z_a)

    def out_finish(i, total):
        out_ref[i] = (
            (fields[i].reshape(tile, ch).astype(F32) + total).astype(BF16).reshape(ny, nz, ch)
        )

    conv(z_a, w2, False, out_finish, 0, nx // 2)
    halo_wait(3, p_g, 1, p_g)
    build(p_g, z_c)
    rows_next(1)
    weight_grad(0, lhs_f, z_c)
    rows_start(0)
    columns_start(1)
    conv(z_a, w2, False, out_finish, nx // 2, nx)

    def field_finish(i, total):
        fgrad_ref[i] = (
            (cot[i].reshape(tile, ch).astype(F32) + total).astype(BF16).reshape(ny, nz, ch)
        )

    conv(z_c, w1, True, field_finish, 0, nx // 2)
    rows_next(0)
    conv(z_c, w1, True, field_finish, nx // 2, nx)
    finish_grad(1, g2_ref)
    columns_start(0)
    finish_grad(0, g1_ref)


def body(sizes, fields, cotangent, first_weight, second_weight):
    ndp, npx, npy = sizes
    batch, nx, ny, nz, ch = fields.shape
    kc = first_weight.shape[0]
    half = ch // npy
    slots = dp_slots(ndp)[1]
    rows = kc // ndp
    rpad = -(-rows // 128) * 128
    wid = ch // (npx * npy)
    cells = nx * ny * nz
    vmem = pl.BlockSpec(memory_space=pltpu.VMEM)
    hbm = pl.BlockSpec(memory_space=pl.ANY)
    padded = pltpu.VMEM((nx + 2, ny + 2, nz, ch), BF16)
    shifted = pltpu.VMEM((nx + 2, ny + 2, nz, 3 * ch), BF16)
    dma = pltpu.SemaphoreType.DMA
    block = (nx, ny, nz, ch)
    out, fgrad, g1, g2 = pl.pallas_call(
        functools.partial(kernel, (ndp, npx, npy, batch * ndp)),
        out_shape=(
            jax.ShapeDtypeStruct(block, BF16),
            jax.ShapeDtypeStruct(block, BF16),
            jax.ShapeDtypeStruct((wid, rpad), F32),
            jax.ShapeDtypeStruct((wid, rpad), F32),
        ),
        in_specs=[vmem, vmem, hbm, hbm],
        out_specs=(vmem, vmem, vmem, vmem),
        scratch_shapes=[
            pltpu.VMEM((kc, ch), BF16),
            pltpu.VMEM((kc, ch), BF16),
            padded, padded, padded, padded,
            shifted, shifted, shifted,
            pltpu.VMEM((ch, cells), BF16),
            pltpu.VMEM((ch, cells), BF16),
            pltpu.VMEM((nx, ny * nz, ch), F32),
            pltpu.VMEM((2, kc, half), F32),
            pltpu.VMEM((2, kc, half), BF16),
            pltpu.VMEM((2, kc, half), BF16),
            pltpu.VMEM((2, len(slots), rows // 2, half), BF16),
            pltpu.VMEM((rpad, half), F32),
            pltpu.VMEM((2, half, rpad), BF16),
            pltpu.VMEM((2, npx, wid, rpad), BF16),
            dma((2,)),
            dma((4, 8)), dma((4, 8)),
            dma((2, 9)), dma((2, 9)),
            dma((2, len(slots))), dma((2, len(slots))),
            dma((2, half // wid)), dma((2, npx)),
        ],
        compiler_params=pltpu.CompilerParams(
            collective_id=0, has_side_effects=True, vmem_limit_bytes=64000000
        ),
        name="closure",
    )(fields.reshape(block), cotangent.reshape(block), first_weight, second_weight)
    out, fgrad, g1, g2 = pl.pallas_call(
        functools.partial(results, rows),
        out_shape=(
            jax.ShapeDtypeStruct(block, BF16),
            jax.ShapeDtypeStruct(block, BF16),
            jax.ShapeDtypeStruct((wid, rows), F32),
            jax.ShapeDtypeStruct((wid, rows), F32),
        ),
        in_specs=[vmem] * 4,
        out_specs=(vmem,) * 4,
        name="results",
    )(out, fgrad, g1, g2)
    return (
        out.reshape(fields.shape),
        fgrad.reshape(fields.shape),
        g1.T,
        g2.T,
    )


def solution(mesh):
    sizes = tuple(mesh.shape[name] for name in ("dp", "px", "py"))
    placed = (P("dp", "px", "py", None, None), P("dp", "px", "py", None, None), P(), P())
    return jax.shard_map(
        functools.partial(body, sizes),
        mesh=mesh,
        in_specs=placed,
        out_specs=(
            P("dp", "px", "py", None, None),
            P("dp", "px", "py", None, None),
            P("dp", ("px", "py")),
            P("dp", ("px", "py")),
        ),
        check_vma=False,
    )
```

profile of v0, /device:TPU:0, one launch (start us, length us, event | category | flops | bytes accessed | tf_op | source)
XLA Modules:
  0.0 75.8 jit_solution(14645990263090221116)
XLA Ops:
  0.6 72.7 %closure.1 = (bf16[4,8,32,256]{3,2,1,0:T(8,128)(2,1)}, bf16[4,8,32,256]{3,2,1,0:T(8,128)(2,1)}, f32[32,1792]{1,0:T(8,128)}, f32[32,1792]{1,0:T(8,128)}) custom-call(bf16[4,8,32,256]{3,2,1,0:T(8,128)(2,1)} %bitcast.6, bf16[4,8,32,256]{3,2,1,0:T(8,128)(2,1)} %bitcast.7, bf16[6912,256]{1,0:T(8,128)(2,1)} %w1_hbm.1, bf16[6912,256]{1,0:T(8,128)(2,1)} %w2_hbm.1), custom_call_target="tpu_custom_call" | custom-call | tf_op jit(solution)/shard_map/closure/pallas_call | solution.py:386
  73.3 2.5 %results.1 = (bf16[4,8,32,256]{3,2,1,0:T(8,128)(2,1)}, bf16[4,8,32,256]{3,2,1,0:T(8,128)(2,1)}, f32[32,1728]{1,0:T(8,128)}, f32[32,1728]{1,0:T(8,128)}) custom-call(bf16[4,8,32,256]{3,2,1,0:T(8,128)(2,1)} %get-tuple-element.12.out_in, bf16[4,8,32,256]{3,2,1,0:T(8,128)(2,1)} %get-tuple-element.13.fgrad_in, f32[32,1792]{1,0:T(8,128)} %get-tuple-element.14.g1_in, ...), custom_call_target="tpu_custom_call" | custom-call | tf_op jit(solution)/shard_map/results/pallas_call | solution.py:422
where the time goes:
time: 77.1 us; the launch traced here: 75.8 us
  Pallas kernels  75.1 us (97%)
    pallas_call x1, Pallas kernels, body(): pl.pallas_call(functools.partial(kernel, (ndp, npx, npy, batch * ndp)), o...  72.7 us
    pallas_call x1, Pallas kernels, body(): pl.pallas_call(functools.partial(results, rows), out_shape=(jax.ShapeDtyp...  2.47 us

commit v1 on v0

--- a/solution.py
+++ b/solution.py
@@ -12,28 +12,51 @@
 DIRS = [(dx, dy) for dx in (-1, 0, 1) for dy in (-1, 0, 1) if dx or dy]
 GELU_C = 0.7978845608028654
 GELU_A = 0.044715
+LAG = 1
 
 
 def gelu_parts(v):
     return jnp.tanh(GELU_C * (v + GELU_A * (v * v * v)))
 
 
-def dp_slots(ndp):
+def reduction_plan(ndp, kc, steps):
     db = 2 if ndp % 2 == 0 else 1
     da = ndp // db
-    first = [(0, 0, hop, item) for hop in range(1, db) for item in [*range(1, da), 0]]
-    other = [(0, 1, hop, item) for hop in range(1, da) for item in [*range(1, db), 0]]
-    slots = [s for pair in zip(first, other) for s in pair]
-    slots += first[len(other) :] + other[len(first) :]
-    slots += [(1, 0, hop, 0) for hop in range(1, da)] + [(1, 1, hop, 0) for hop in range(1, db)]
-    return (da, db), slots
-
-
-def results(rows, out_in, fgrad_in, g1_in, g2_in, out_ref, fgrad_ref, g1_ref, g2_ref):
-    out_ref[...] = out_in[...]
-    fgrad_ref[...] = fgrad_in[...]
-    g1_ref[...] = g1_in[:, :rows]
-    g2_ref[...] = g2_in[:, :rows]
+    rows = kc // ndp
+    hops = [(ha, hb) for ha in range(1, da) for hb in range(1, db)]
+    hops += [(0, hb) for hb in range(1, db)] + [(ha, 0) for ha in range(1, da)] + [(0, 0)]
+    each = kc // steps
+    codes, done = [], [0] * ndp
+    for d in range(ndp):
+        order = []
+        for k, (ha, hb) in enumerate(hops):
+            p = (d // db + ha) % da * db + (d % db + hb) % db
+            for step in range(p * rows // each, -(-(p + 1) * rows // each)):
+                if step not in order:
+                    order.append(step)
+            done[k] = max(done[k], len(order))
+        codes.append(sum(step * steps**t for t, step in enumerate(order)))
+    first = -(-rows // 256) * 128
+    chunks = []
+    for side, (low, high) in enumerate(((0, first), (first, rows))):
+        middle = low + -(-(high - low) // 256) * 128
+        for start, stop in ((low, middle), (middle, high)):
+            if stop > start:
+                chunks.append((side, start, start - low, stop - start))
+    return (da, db), hops, codes, done, chunks
+
+
+def slot_count(da, db):
+    return (db - 1) * da + (da - 1) * db + da - 1 + db - 1
+
+
+def results(*refs):
+    ins, outs, sems = refs[:4], refs[4:8], refs[8]
+    copies = [pltpu.make_async_copy(ins[i], outs[i], sems.at[i]) for i in range(4)]
+    for copy in copies:
+        copy.start()
+    for copy in copies:
+        copy.wait()
 
 
 def kernel(
@@ -41,16 +64,16 @@
     fields, cot, w1_hbm, w2_hbm,
     out_ref, fgrad_ref, g1_ref, g2_ref,
     w1, w2, p_f, p_c, p_h, p_g, z_a, z_b, z_c, lhs_f, lhs_h, pre,
-    own, send_a, recv_a, recv_b, tot, send_z, recv_z,
+    own, send_a, recv_a, recv_b, send_z, recv_z,
     sem_w, halo_send, halo_recv, a_send, a_recv, b_send, b_recv, z_send, z_recv,
 ):
     ndp, npx, npy, rollouts = sizes
-    factors, b_slots = dp_slots(ndp)
     nx, ny, nz, ch = fields.shape
     cells = nx * ny * nz
     half = ch // npy
-    rows = own.shape[1] // ndp
-    rpad = tot.shape[0]
+    kc = own.shape[1]
+    rows = kc // ndp
+    (da, db), hops, codes, done, chunks = reduction_plan(ndp, kc, 9)
     wid = recv_z.shape[2]
     nj = half // wid
     d, x, y = lax.axis_index("dp"), lax.axis_index("px"), lax.axis_index("py")
@@ -173,10 +196,67 @@
             device_id_type=MESH,
         )
 
+    ia, ib = d // db, lax.rem(d, db)
+    code = jnp.int32(codes[0])
+    for i in range(1, ndp):
+        code = jnp.where(d == i, jnp.int32(codes[i]), code)
+
+    def ring(index, hop, count):
+        return lax.rem(index + hop, count) if hop else index
+
+    def piece(ha, hb, chunk):
+        first = (ring(ia, ha, da) * db + ring(ib, hb, db)) * rows + chunks[chunk][1]
+        return pl.ds(pl.multiple_of(first, 16), chunks[chunk][3])
+
+    def slot_of(phase, side, ha, hb):
+        if phase == 0:
+            return (hb - 1) * da + ha if side == 0 else (db - 1) * da + (ha - 1) * db + hb
+        base = (db - 1) * da + (da - 1) * db
+        return base + ha - 1 if side == 0 else base + da - 1 + hb - 1
+
+    def b_copy(which, phase, ha, hb, chunk):
+        side, _, offset, size = chunks[chunk]
+        if (side == 0) == (phase == 0):
+            peer = ia * db + ring(ib, hb, db)
+        else:
+            peer = ring(ia, ha, da) * db + ib
+        slot = slot_of(phase, side, ha, hb)
+        return pltpu.make_async_remote_copy(
+            src_ref=send_a.at[which, piece(ha, hb, chunk)],
+            dst_ref=recv_b.at[which, slot, pl.ds(offset, size)],
+            send_sem=b_send.at[which, slot, chunk],
+            recv_sem=b_recv.at[which, slot, chunk],
+            device_id=(peer, x, y),
+            device_id_type=MESH,
+        )
+
+    def arrived(which, phase, ha, hb, chunk):
+        side, _, offset, size = chunks[chunk]
+        b_copy(which, phase, ha, hb, chunk).wait_recv()
+        return recv_b[which, slot_of(phase, side, ha, hb), pl.ds(offset, size)].astype(F32)
+
+    def piece_start(which, k):
+        for t in range(done[k - 1] if k else 0, done[k]):
+            a_copy(which, lax.rem(code // 9**t, 9)).wait()
+        ha, hb = hops[k]
+        for chunk, (side, _, _, _) in enumerate(chunks):
+            part = piece(ha, hb, chunk)
+            total = own[which, part] + recv_a[which, part].astype(F32)
+            if (hb if side == 0 else ha) > 0:
+                send_a[which, part] = total.astype(BF16)
+                b_copy(which, 0, ha, hb, chunk).start()
+            else:
+                own[which, part] = total
+
     def weight_grad(which, lhs, shifted):
-        @pl.loop(0, 9)
-        def _(step):
-            a, b = step // 3, step % 3
+        def one(t, left):
+            for k in range(len(hops)):
+                if done[k] + LAG < 9:
+                    @pl.when(t == done[k] + LAG)
+                    def _():
+                        piece_start(which, k)
+            step = lax.rem(left, 9)
+            a, b = step // 3, lax.rem(step, 3)
             rhs = shifted[pl.ds(2 - a, nx), pl.ds(2 - b, ny)].reshape(cells, 3 * ch)
             prod = jnp.dot(lhs[...], rhs, preferred_element_type=F32)
             for c in range(3):
@@ -186,123 +266,97 @@
                 own[which, here] = jnp.where(y == 0, low, high)
                 send_a[which, here] = jnp.where(y == 0, high, low).astype(BF16)
             a_copy(which, step).start()
-
-    da, db = factors
-    part_rows = rows // 2
-    ia, ib = d // db, lax.rem(d, db)
-
-    def piece(a, b, side):
-        first = (a * db + b) * rows + side * part_rows
-        return pl.ds(pl.multiple_of(first, 16), part_rows)
-
-    def ring(index, hop, count):
-        return lax.rem(index + hop, count)
-
-    def b_copy(which, phase, side, hop, item):
-        along_b = (side == 0) == (phase == 0)
-        if along_b:
-            a, b = (ring(ia, item, da) if phase == 0 else ia), ring(ib, hop, db)
-            peer = ia * db + b
-        else:
-            a, b = ring(ia, hop, da), (ring(ib, item, db) if phase == 0 else ib)
-            peer = a * db + ib
-        slot = b_slots.index((phase, side, hop, item))
-        return piece(a, b, side), pltpu.make_async_remote_copy(
-            src_ref=send_a.at[which, piece(a, b, side)],
-            dst_ref=recv_b.at[which, slot],
-            send_sem=b_send.at[which, slot],
-            recv_sem=b_recv.at[which, slot],
-            device_id=(peer, x, y),
-            device_id_type=MESH,
-        )
-
-    def rows_start(which):
-        @pl.loop(0, 9)
-        def _(step):
-            a_copy(which, step).wait()
-
-        for slot in [s for s in b_slots if s[0] == 0]:
-            part, copy = b_copy(which, *slot)
-            send_a[which, part] = (own[which, part] + recv_a[which, part].astype(F32)).astype(BF16)
-            copy.start()
-        for side, count in ((0, da), (1, db)):
-            for item in range(count):
-                a, b = (ring(ia, item, da), ib) if side == 0 else (ia, ring(ib, item, db))
-                part = piece(a, b, side)
-                own[which, part] = own[which, part] + recv_a[which, part].astype(F32)
-
-    def rows_next(which):
-        for side, count, hops in ((0, da, db), (1, db, da)):
-            for item in [*range(1, count), 0]:
-                a, b = (ring(ia, item, da), ib) if side == 0 else (ia, ring(ib, item, db))
-                part = piece(a, b, side)
-                total = own[which, part]
-                for hop in range(1, hops):
-                    slot = (0, side, hop, item)
-                    b_copy(which, *slot)[1].wait()
-                    total = total + recv_b[which, b_slots.index(slot)].astype(F32)
-                if item:
-                    send_a[which, part] = total.astype(BF16)
-                    b_copy(which, 1, side, item, 0)[1].start()
-                else:
-                    own[which, part] = total
+            return left // 9
+
+        lax.fori_loop(0, 9, one, code)
+
+    def pieces_rest(which):
+        for k in range(len(hops)):
+            if done[k] + LAG >= 9:
+                piece_start(which, k)
+
+    def relay(which, chunk):
+        side = chunks[chunk][0]
+        for hop in range(1, da if side == 0 else db):
+            ha, hb = (hop, 0) if side == 0 else (0, hop)
+            part = piece(ha, hb, chunk)
+            total = own[which, part]
+            for first in range(1, db if side == 0 else da):
+                fa, fb = (hop, first) if side == 0 else (first, hop)
+                total = total + arrived(which, 0, fa, fb, chunk)
+            send_a[which, part] = total.astype(BF16)
+            b_copy(which, 1, ha, hb, chunk).start()
 
     def z_ids(j):
         owner = y * nj + j
         return owner // npy, lax.rem(owner, npy)
 
-    def z_remote(which, j):
+    def lanes(chunk):
+        return pl.ds(chunks[chunk][1], -(-chunks[chunk][3] // 128) * 128)
+
+    def z_remote(which, j, chunk):
         px_o, py_o = z_ids(j)
         return pltpu.make_async_remote_copy(
-            src_ref=send_z.at[which, pl.ds(j * wid, wid)],
-            dst_ref=recv_z.at[which, x],
-            send_sem=z_send.at[which, j],
-            recv_sem=z_recv.at[which, x],
+            src_ref=send_z.at[which, pl.ds(j * wid, wid), lanes(chunk)],
+            dst_ref=recv_z.at[which, x, :, lanes(chunk)],
+            send_sem=z_send.at[which, j, chunk],
+            recv_sem=z_recv.at[which, x, chunk],
             device_id=(d, px_o, py_o),
             device_id_type=MESH,
         )
 
-    def columns_start(which):
-        for side, hops in ((0, da), (1, db)):
-            total = own[which, piece(ia, ib, side)]
-            for hop in range(1, hops):
-                slot = (1, side, hop, 0)
-                b_copy(which, *slot)[1].wait()
-                total = total + recv_b[which, b_slots.index(slot)].astype(F32)
-            tot[side * part_rows : (side + 1) * part_rows] = total
-        if rpad > rows:
-            tot[rows:rpad] = jnp.zeros((rpad - rows, half), F32)
-        send_z[which] = tot[...].T.astype(BF16)
+    def columns_start(which, chunk):
+        side, _, _, size = chunks[chunk]
+        total = own[which, piece(0, 0, chunk)]
+        for hop in range(1, db if side == 0 else da):
+            total = total + arrived(which, 0, *((0, hop) if side == 0 else (hop, 0)), chunk)
+        for hop in range(1, da if side == 0 else db):
+            total = total + arrived(which, 1, *((hop, 0) if side == 0 else (0, hop)), chunk)
+        pad = -size % 128
+        if pad:
+            total = jnp.concatenate([total, jnp.zeros((pad, half), F32)], axis=0)
+        send_z[which, :, lanes(chunk)] = total.T.astype(BF16)
         for j in range(nj):
             px_o, py_o = z_ids(j)
             mine = (px_o == x) & (py_o == y)
 
             @pl.when(jnp.logical_not(mine))
             def _():
-                z_remote(which, j).start()
+                z_remote(which, j, chunk).start()
 
             @pl.when(mine)
             def _():
                 pltpu.make_async_copy(
-                    send_z.at[which, pl.ds(j * wid, wid)], recv_z.at[which, x], z_recv.at[which, x]
+                    send_z.at[which, pl.ds(j * wid, wid), lanes(chunk)],
+                    recv_z.at[which, x, :, lanes(chunk)],
+                    z_recv.at[which, x, chunk],
                 ).start()
 
-    def finish_grad(which, grad):
-        for j in range(nj):
-            px_o, py_o = z_ids(j)
-
-            @pl.when(jnp.logical_not((px_o == x) & (py_o == y)))
-            def _():
-                z_remote(which, j).wait_send()
-
+    def finish_grad(which, grad, chunk):
         total = None
         for i in range(npx):
-            pltpu.make_async_copy(
-                recv_z.at[which, i], recv_z.at[which, i], z_recv.at[which, i]
-            ).wait()
-            term = recv_z[which, i].astype(F32)
+            here = recv_z.at[which, i, :, lanes(chunk)]
+            pltpu.make_async_copy(here, here, z_recv.at[which, i, chunk]).wait()
+            term = recv_z[which, i, :, lanes(chunk)].astype(F32)
             total = term if total is None else total + term
-        grad[...] = total / rollouts
+        _, start, _, size = chunks[chunk]
+        grad[:, start : start + size] = (total / rollouts)[:, :size]
+
+    def sent(which):
+        for chunk, (side, _, _, _) in enumerate(chunks):
+            for ha, hb in hops:
+                if (hb if side == 0 else ha) > 0:
+                    b_copy(which, 0, ha, hb, chunk).wait_send()
+            for hop in range(1, da if side == 0 else db):
+                b_copy(which, 1, *((hop, 0) if side == 0 else (0, hop)), chunk).wait_send()
+            for j in range(nj):
+                px_o, py_o = z_ids(j)
+
+                @pl.when(jnp.logical_not((px_o == x) & (py_o == y)))
+                def _():
+                    z_remote(which, j, chunk).wait_send()
+
+    every = range(len(chunks))
 
     halo_start(0, fields, 0, p_f)
     halo_start(1, cot, 0, p_c)
@@ -324,7 +378,7 @@
     halo_wait(1, cot, 0, p_c)
     build(p_c, z_b)
     weight_grad(1, lhs_h, z_b)
-    rows_start(1)
+    pieces_rest(1)
     load_w[1].wait()
 
     def grad_finish(i, total):
@@ -337,6 +391,8 @@
 
     conv(z_b, w2, True, grad_finish)
     halo_start(3, p_g, 1, p_g)
+    for chunk in every:
+        relay(1, chunk)
     halo_wait(2, p_h, 1, p_h)
     build(p_h, z_a)
 
@@ -348,10 +404,10 @@
     conv(z_a, w2, False, out_finish, 0, nx // 2)
     halo_wait(3, p_g, 1, p_g)
     build(p_g, z_c)
-    rows_next(1)
     weight_grad(0, lhs_f, z_c)
-    rows_start(0)
-    columns_start(1)
+    pieces_rest(0)
+    for chunk in every:
+        columns_start(1, chunk)
     conv(z_a, w2, False, out_finish, nx // 2, nx)
 
     def field_finish(i, total):
@@ -360,11 +416,17 @@
         )
 
     conv(z_c, w1, True, field_finish, 0, nx // 2)
-    rows_next(0)
+    for chunk in every:
+        relay(0, chunk)
     conv(z_c, w1, True, field_finish, nx // 2, nx)
-    finish_grad(1, g2_ref)
-    columns_start(0)
-    finish_grad(0, g1_ref)
+    for chunk in every:
+        finish_grad(1, g2_ref, chunk)
+    sent(1)
+    for chunk in every:
+        columns_start(0, chunk)
+    for chunk in every:
+        finish_grad(0, g1_ref, chunk)
+    sent(0)
 
 
 def body(sizes, fields, cotangent, first_weight, second_weight):
@@ -372,7 +434,9 @@
     batch, nx, ny, nz, ch = fields.shape
     kc = first_weight.shape[0]
     half = ch // npy
-    slots = dp_slots(ndp)[1]
+    (da, db), _, _, _, chunks = reduction_plan(ndp, kc, 9)
+    slots = slot_count(da, db)
+    longest = max(offset + size for _, _, offset, size in chunks)
     rows = kc // ndp
     rpad = -(-rows // 128) * 128
     wid = ch // (npx * npy)
@@ -388,8 +452,8 @@
         out_shape=(
             jax.ShapeDtypeStruct(block, BF16),
             jax.ShapeDtypeStruct(block, BF16),
-            jax.ShapeDtypeStruct((wid, rpad), F32),
-            jax.ShapeDtypeStruct((wid, rpad), F32),
+            jax.ShapeDtypeStruct((wid, rows), F32),
+            jax.ShapeDtypeStruct((wid, rows), F32),
         ),
         in_specs=[vmem, vmem, hbm, hbm],
         out_specs=(vmem, vmem, vmem, vmem),
@@ -404,15 +468,14 @@
             pltpu.VMEM((2, kc, half), F32),
             pltpu.VMEM((2, kc, half), BF16),
             pltpu.VMEM((2, kc, half), BF16),
-            pltpu.VMEM((2, len(slots), rows // 2, half), BF16),
-            pltpu.VMEM((rpad, half), F32),
+            pltpu.VMEM((2, slots, longest, half), BF16),
             pltpu.VMEM((2, half, rpad), BF16),
             pltpu.VMEM((2, npx, wid, rpad), BF16),
             dma((2,)),
             dma((4, 8)), dma((4, 8)),
             dma((2, 9)), dma((2, 9)),
-            dma((2, len(slots))), dma((2, len(slots))),
-            dma((2, half // wid)), dma((2, npx)),
+            dma((2, slots, len(chunks))), dma((2, slots, len(chunks))),
+            dma((2, half // wid, len(chunks))), dma((2, npx, len(chunks))),
         ],
         compiler_params=pltpu.CompilerParams(
             collective_id=0, has_side_effects=True, vmem_limit_bytes=64000000
@@ -420,15 +483,16 @@
         name="closure",
     )(fields.reshape(block), cotangent.reshape(block), first_weight, second_weight)
     out, fgrad, g1, g2 = pl.pallas_call(
-        functools.partial(results, rows),
+        results,
         out_shape=(
             jax.ShapeDtypeStruct(block, BF16),
             jax.ShapeDtypeStruct(block, BF16),
             jax.ShapeDtypeStruct((wid, rows), F32),
             jax.ShapeDtypeStruct((wid, rows), F32),
         ),
-        in_specs=[vmem] * 4,
-        out_specs=(vmem,) * 4,
+        in_specs=[hbm] * 4,
+        out_specs=(hbm,) * 4,
+        scratch_shapes=[dma((4,))],
         name="results",
     )(out, fgrad, g1, g2)
     return (

time: 77.1 us -> 119 us (1.54); the launches traced: 75.8 us -> 119 us
  Pallas kernels: 75.1 us -> 118 us
    pallas_call x1, Pallas kernels: 2.47 us -> 46.8 us  [body(): pl.pallas_call(results, out_shape=(jax.ShapeDtypeStruct(block, BF16), jax...]
where the time goes in v1:
time: 119 us
  Pallas kernels  118 us (99%)
    pallas_call x1, Pallas kernels, body(): pl.pallas_call(functools.partial(kernel, (ndp, npx, npy, batch * ndp)), o...  71.6 us
    pallas_call x1, Pallas kernels, body(): pl.pallas_call(results, out_shape=(jax.ShapeDtypeStruct(block, BF16), jax...  46.8 us

profile of v1, /device:TPU:0, one launch (start us, length us, event | category | flops | bytes accessed | tf_op | source)
XLA Modules:
  0.0 119.1 jit_solution(16760643269726530070)
XLA Ops:
  0.6 71.6 %closure.1 = (bf16[4,8,32,256]{3,2,1,0:T(8,128)(2,1)}, bf16[4,8,32,256]{3,2,1,0:T(8,128)(2,1)}, f32[32,1728]{1,0:T(8,128)}, f32[32,1728]{1,0:T(8,128)}) custom-call(bf16[4,8,32,256]{3,2,1,0:T(8,128)(2,1)} %bitcast.6, bf16[4,8,32,256]{3,2,1,0:T(8,128)(2,1)} %bitcast.7, bf16[6912,256]{1,0:T(8,128)(2,1)} %w1_hbm.1, bf16[6912,256]{1,0:T(8,128)(2,1)} %w2_hbm.1), custom_call_target="tpu_custom_call" | custom-call | tf_op jit(solution)/shard_map/closure/pallas_call | solution.py:450
  72.3 46.8 %results.1 = (bf16[4,8,32,256]{3,2,1,0:T(8,128)(2,1)}, bf16[4,8,32,256]{3,2,1,0:T(8,128)(2,1)}, f32[32,1728]{1,0:T(8,128)}, f32[32,1728]{1,0:T(8,128)}) custom-call(bf16[4,8,32,256]{3,2,1,0:T(8,128)(2,1)} %get-tuple-element.12.refs_0_, bf16[4,8,32,256]{3,2,1,0:T(8,128)(2,1)} %get-tuple-element.13.refs_1_, f32[32,1728]{1,0:T(8,128)} %get-tuple-element.14.refs_2_, ...), custom_call_target="tpu_custom_call" | custom-call | tf_op jit(solution)/shard_map/results/pallas_call | solution.py:485

commit v2 on v1

--- a/solution.py
+++ b/solution.py
@@ -10,9 +10,11 @@
 MESH = pl.DeviceIdType.MESH
 F32, BF16 = jnp.float32, jnp.bfloat16
 DIRS = [(dx, dy) for dx in (-1, 0, 1) for dy in (-1, 0, 1) if dx or dy]
+ALONG = [i for i, (dx, _) in enumerate(DIRS) if dx]
+ACROSS = [i for i, (dx, _) in enumerate(DIRS) if not dx]
 GELU_C = 0.7978845608028654
 GELU_A = 0.044715
-LAG = 1
+LAG = 2
 
 
 def gelu_parts(v):
@@ -39,10 +41,12 @@
     first = -(-rows // 256) * 128
     chunks = []
     for side, (low, high) in enumerate(((0, first), (first, rows))):
-        middle = low + -(-(high - low) // 256) * 128
-        for start, stop in ((low, middle), (middle, high)):
-            if stop > start:
-                chunks.append((side, start, start - low, stop - start))
+        tiles, start = -(-(high - low) // 128), low
+        for left in range(min(3, tiles), 0, -1):
+            stop = min(high, start + -(-tiles // left) * 128)
+            tiles -= -(-tiles // left)
+            chunks.append((side, start, start - low, stop - start))
+            start = stop
     return (da, db), hops, codes, done, chunks
 
 
@@ -74,15 +78,18 @@
     kc = own.shape[1]
     rows = kc // ndp
     (da, db), hops, codes, done, chunks = reduction_plan(ndp, kc, 9)
-    wid = recv_z.shape[2]
+    wid = recv_z[0].shape[2]
     nj = half // wid
     d, x, y = lax.axis_index("dp"), lax.axis_index("px"), lax.axis_index("py")
 
+    inner = pl.ds(1, nx), pl.ds(1, ny)
+    load_f = pltpu.make_async_copy(fields, p_f.at[inner], sem_w.at[2])
+    load_c = pltpu.make_async_copy(cot, p_c.at[inner], sem_w.at[3])
     load_w = [
         pltpu.make_async_copy(w1_hbm, w1, sem_w.at[0]),
         pltpu.make_async_copy(w2_hbm, w2, sem_w.at[1]),
     ]
-    for copy in load_w:
+    for copy in [load_f, load_c, *load_w]:
         copy.start()
 
     barrier = pltpu.get_barrier_semaphore()
@@ -121,8 +128,10 @@
             device_id_type=MESH,
         )
 
-    def halo_start(which, src, base, padded):
-        for index, (dx, dy) in enumerate(DIRS):
+    def halo_start(which, src, base, padded, group):
+        for index in group:
+            dx, dy = DIRS[index]
+
             @pl.when(exists(dx, dy))
             def _():
                 halo_copy(which, src, base, padded, index).start()
@@ -132,8 +141,10 @@
                 sx, sy = span_dst(dx, nx), span_dst(dy, ny)
                 padded[sx, sy] = jnp.zeros((sx.size, sy.size, nz, ch), BF16)
 
-    def halo_wait(which, src, base, padded):
-        for index, (dx, dy) in enumerate(DIRS):
+    def halo_wait(which, src, base, padded, group):
+        for index in group:
+            dx, dy = DIRS[index]
+
             @pl.when(exists(dx, dy))
             def _():
                 halo_copy(which, src, base, padded, index).wait_send()
@@ -142,23 +153,27 @@
             def _():
                 halo_copy(which, src, base, padded, index).wait_recv()
 
-    def build(padded, shifted):
-        @pl.loop(0, nx + 2)
-        def _(i):
+    def build(padded, shifted, low, high, stride=1):
+        @pl.loop(low, high)
+        def _(j):
+            i = j * stride
             plane = padded[i]
             flat = plane.reshape((ny + 2) * nz, ch).astype(F32)
             place = lax.broadcasted_iota(jnp.int32, flat.shape, 0) % nz
-            low = jnp.where(place == 0, 0.0, pltpu.roll(flat, 1, 0))
-            high = jnp.where(place == nz - 1, 0.0, pltpu.roll(flat, flat.shape[0] - 1, 0))
-            shifted[i, :, :, 0:ch] = low.astype(BF16).reshape(plane.shape)
+            before = jnp.where(place == 0, 0.0, pltpu.roll(flat, 1, 0))
+            after = jnp.where(place == nz - 1, 0.0, pltpu.roll(flat, flat.shape[0] - 1, 0))
+            shifted[i, :, :, 0:ch] = before.astype(BF16).reshape(plane.shape)
             shifted[i, :, :, ch : 2 * ch] = plane
-            shifted[i, :, :, 2 * ch : 3 * ch] = high.astype(BF16).reshape(plane.shape)
+            shifted[i, :, :, 2 * ch : 3 * ch] = after.astype(BF16).reshape(plane.shape)
 
     tile = ny * nz
 
-    def conv(shifted, weight, flipped, finish, low=0, high=nx):
-        @pl.loop(low, high)
-        def _(i):
+    def conv(shifted, weight, flipped, finish, *planes):
+        step = planes[1] - planes[0] if len(planes) > 1 else 1
+
+        @pl.loop(0, len(planes))
+        def _(j):
+            i = planes[0] + j * step
             total = None
             for a in range(3):
                 for b in range(3):
@@ -183,6 +198,7 @@
                         total = term if total is None else total + term
             finish(i, total)
 
+    edges, middle = sorted({0, nx - 1}), range(1, nx - 1)
     partner = 1 - y
 
     def a_copy(which, step):
@@ -197,6 +213,11 @@
         )
 
     ia, ib = d // db, lax.rem(d, db)
+    groups = [[], [], []]
+    for side in range(2):
+        here = [chunk for chunk in range(len(chunks)) if chunks[chunk][0] == side]
+        for order, chunk in enumerate(here):
+            groups[order].append(chunk)
     code = jnp.int32(codes[0])
     for i in range(1, ndp):
         code = jnp.where(d == i, jnp.int32(codes[i]), code)
@@ -244,12 +265,25 @@
             total = own[which, part] + recv_a[which, part].astype(F32)
             if (hb if side == 0 else ha) > 0:
                 send_a[which, part] = total.astype(BF16)
-                b_copy(which, 0, ha, hb, chunk).start()
+                if chunk in groups[0] or (ha and hb and chunk in groups[1]):
+                    b_copy(which, 0, ha, hb, chunk).start()
             else:
                 own[which, part] = total
 
-    def weight_grad(which, lhs, shifted):
+    def pieces_send(which, diagonal, order):
+        for ha, hb in hops:
+            if order < len(groups) and (ha > 0 and hb > 0) == diagonal:
+                for chunk in groups[order]:
+                    if (hb if chunks[chunk][0] == 0 else ha) > 0:
+                        b_copy(which, 0, ha, hb, chunk).start()
+
+    def weight_grad(which, lhs, shifted, beside):
         def one(t, left):
+            for at, task in beside:
+                @pl.when(t == at)
+                def _():
+                    task()
+
             for k in range(len(hops)):
                 if done[k] + LAG < 9:
                     @pl.when(t == done[k] + LAG)
@@ -272,8 +306,17 @@
 
     def pieces_rest(which):
         for k in range(len(hops)):
-            if done[k] + LAG >= 9:
+            if done[k] + LAG >= 9 and k < len(hops) - 1:
                 piece_start(which, k)
+
+    def own_piece(which):
+        piece_start(which, len(hops) - 1)
+
+    def advance(which, order):
+        for chunk in groups[order]:
+            relay(which, chunk)
+        pieces_send(which, True, order + 2)
+        pieces_send(which, False, order + 1)
 
     def relay(which, chunk):
         side = chunks[chunk][0]
@@ -291,14 +334,11 @@
         owner = y * nj + j
         return owner // npy, lax.rem(owner, npy)
 
-    def lanes(chunk):
-        return pl.ds(chunks[chunk][1], -(-chunks[chunk][3] // 128) * 128)
-
     def z_remote(which, j, chunk):
         px_o, py_o = z_ids(j)
         return pltpu.make_async_remote_copy(
-            src_ref=send_z.at[which, pl.ds(j * wid, wid), lanes(chunk)],
-            dst_ref=recv_z.at[which, x, :, lanes(chunk)],
+            src_ref=send_z[chunk].at[which, pl.ds(j * wid, wid)],
+            dst_ref=recv_z[chunk].at[which, x],
             send_sem=z_send.at[which, j, chunk],
             recv_sem=z_recv.at[which, x, chunk],
             device_id=(d, px_o, py_o),
@@ -315,7 +355,7 @@
         pad = -size % 128
         if pad:
             total = jnp.concatenate([total, jnp.zeros((pad, half), F32)], axis=0)
-        send_z[which, :, lanes(chunk)] = total.T.astype(BF16)
+        send_z[chunk][which] = total.T.astype(BF16)
         for j in range(nj):
             px_o, py_o = z_ids(j)
             mine = (px_o == x) & (py_o == y)
@@ -326,18 +366,22 @@
 
             @pl.when(mine)
             def _():
-                pltpu.make_async_copy(
-                    send_z.at[which, pl.ds(j * wid, wid), lanes(chunk)],
-                    recv_z.at[which, x, :, lanes(chunk)],
-                    z_recv.at[which, x, chunk],
-                ).start()
+                recv_z[chunk][which, x] = send_z[chunk][which, j * wid : (j + 1) * wid]
+
+    def columns_send(which, order):
+        for chunk in groups[order]:
+            columns_start(which, chunk)
 
     def finish_grad(which, grad, chunk):
         total = None
         for i in range(npx):
-            here = recv_z.at[which, i, :, lanes(chunk)]
-            pltpu.make_async_copy(here, here, z_recv.at[which, i, chunk]).wait()
-            term = recv_z[which, i, :, lanes(chunk)].astype(F32)
+            here = recv_z[chunk].at[which, i]
+
+            @pl.when((x != i) | (y != (x * npy + y) // nj))
+            def _():
+                pltpu.make_async_copy(here, here, z_recv.at[which, i, chunk]).wait()
+
+            term = recv_z[chunk][which, i].astype(F32)
             total = term if total is None else total + term
         _, start, _, size = chunks[chunk]
         grad[:, start : start + size] = (total / rollouts)[:, :size]
@@ -358,27 +402,35 @@
 
     every = range(len(chunks))
 
-    halo_start(0, fields, 0, p_f)
-    halo_start(1, cot, 0, p_c)
-    p_f[pl.ds(1, nx), pl.ds(1, ny)] = fields[...]
-    p_c[pl.ds(1, nx), pl.ds(1, ny)] = cot[...]
-    lhs_f[...] = fields[...].reshape(cells, ch).T
-    halo_wait(0, fields, 0, p_f)
-    build(p_f, z_a)
-    load_w[0].wait()
+    load_f.wait()
+    halo_start(0, p_f, 1, p_f, ALONG)
+    halo_start(0, p_f, 1, p_f, ACROSS)
+    load_c.wait()
+    halo_start(1, p_c, 1, p_c, ACROSS)
+    halo_wait(0, p_f, 1, p_f, ACROSS)
+    build(p_f, z_a, 1, nx + 1)
 
     def hidden_finish(i, total):
         pre[i] = total
         value = (total * (0.5 * (1.0 + gelu_parts(total)))).astype(BF16)
         p_h[i + 1, pl.ds(1, ny)] = value.reshape(ny, nz, ch)
 
-    conv(z_a, w1, False, hidden_finish)
-    halo_start(2, p_h, 1, p_h)
+    load_w[0].wait()
+    conv(z_a, w1, False, hidden_finish, *middle)
+    halo_start(1, p_c, 1, p_c, ALONG)
+    halo_wait(1, p_c, 1, p_c, ACROSS)
+    build(p_c, z_b, 1, nx + 1)
+    halo_wait(0, p_f, 1, p_f, ALONG)
+    build(p_f, z_a, 0, 2, nx + 1)
+    conv(z_a, w1, False, hidden_finish, *edges)
+    halo_start(2, p_h, 1, p_h, ALONG)
+    halo_start(2, p_h, 1, p_h, ACROSS)
     lhs_h[...] = p_h[pl.ds(1, nx), pl.ds(1, ny)].reshape(cells, ch).T
-    halo_wait(1, cot, 0, p_c)
-    build(p_c, z_b)
-    weight_grad(1, lhs_h, z_b)
+    halo_wait(1, p_c, 1, p_c, ALONG)
+    build(p_c, z_b, 0, 2, nx + 1)
+    weight_grad(1, lhs_h, z_b, [])
     pieces_rest(1)
+    advance(1, 0)
     load_w[1].wait()
 
     def grad_finish(i, total):
@@ -389,42 +441,54 @@
         )
         p_g[i + 1, pl.ds(1, ny)] = (total * slope).astype(BF16).reshape(ny, nz, ch)
 
-    conv(z_b, w2, True, grad_finish)
-    halo_start(3, p_g, 1, p_g)
-    for chunk in every:
-        relay(1, chunk)
-    halo_wait(2, p_h, 1, p_h)
-    build(p_h, z_a)
+    conv(z_b, w2, True, grad_finish, *edges)
+    halo_start(3, p_g, 1, p_g, ALONG)
+    own_piece(1)
+    advance(1, 1)
+    conv(z_b, w2, True, grad_finish, *middle)
+    halo_start(3, p_g, 1, p_g, ACROSS)
+    lhs_f[...] = p_f[inner].reshape(cells, ch).T
+    halo_wait(2, p_h, 1, p_h, ALONG)
+    halo_wait(2, p_h, 1, p_h, ACROSS)
+    build(p_h, z_a, 0, nx + 2)
+    columns_send(1, 0)
 
     def out_finish(i, total):
         out_ref[i] = (
-            (fields[i].reshape(tile, ch).astype(F32) + total).astype(BF16).reshape(ny, nz, ch)
-        )
-
-    conv(z_a, w2, False, out_finish, 0, nx // 2)
-    halo_wait(3, p_g, 1, p_g)
-    build(p_g, z_c)
-    weight_grad(0, lhs_f, z_c)
+            (p_f[i + 1, pl.ds(1, ny)].reshape(tile, ch).astype(F32) + total).astype(BF16).reshape(ny, nz, ch)
+        )
+
+    conv(z_a, w2, False, out_finish, *range(nx // 2))
+    advance(1, 2)
+    halo_wait(3, p_g, 1, p_g, ACROSS)
+    build(p_g, z_c, 1, nx + 1)
+    halo_wait(3, p_g, 1, p_g, ALONG)
+    build(p_g, z_c, 0, 2, nx + 1)
+    weight_grad(
+        0, lhs_f, z_c,
+        [(1, lambda: columns_send(1, 1)), (7, lambda: columns_send(1, 2))],
+    )
     pieces_rest(0)
-    for chunk in every:
-        columns_start(1, chunk)
-    conv(z_a, w2, False, out_finish, nx // 2, nx)
+    advance(0, 0)
+    conv(z_a, w2, False, out_finish, *range(nx // 2, nx))
+    own_piece(0)
+    advance(0, 1)
 
     def field_finish(i, total):
         fgrad_ref[i] = (
-            (cot[i].reshape(tile, ch).astype(F32) + total).astype(BF16).reshape(ny, nz, ch)
-        )
-
-    conv(z_c, w1, True, field_finish, 0, nx // 2)
-    for chunk in every:
-        relay(0, chunk)
-    conv(z_c, w1, True, field_finish, nx // 2, nx)
+            (p_c[i + 1, pl.ds(1, ny)].reshape(tile, ch).astype(F32) + total).astype(BF16).reshape(ny, nz, ch)
+        )
+
+    conv(z_c, w1, True, field_finish, *edges)
+    columns_send(0, 0)
+    advance(0, 2)
+    conv(z_c, w1, True, field_finish, *middle)
     for chunk in every:
         finish_grad(1, g2_ref, chunk)
     sent(1)
-    for chunk in every:
-        columns_start(0, chunk)
-    for chunk in every:
+    columns_send(0, 1)
+    columns_send(0, 2)
+    for chunk in groups[0] + groups[1] + groups[2]:
         finish_grad(0, g1_ref, chunk)
     sent(0)
 
@@ -438,11 +502,12 @@
     slots = slot_count(da, db)
     longest = max(offset + size for _, _, offset, size in chunks)
     rows = kc // ndp
-    rpad = -(-rows // 128) * 128
+    widths = [-(-size // 128) * 128 for _, _, _, size in chunks]
     wid = ch // (npx * npy)
     cells = nx * ny * nz
     vmem = pl.BlockSpec(memory_space=pltpu.VMEM)
-    hbm = pl.BlockSpec(memory_space=pl.ANY)
+    hbm = pl.BlockSpec(memory_space=pltpu.HBM)
+    anywhere = pl.BlockSpec(memory_space=pl.ANY)
     padded = pltpu.VMEM((nx + 2, ny + 2, nz, ch), BF16)
     shifted = pltpu.VMEM((nx + 2, ny + 2, nz, 3 * ch), BF16)
     dma = pltpu.SemaphoreType.DMA
@@ -455,7 +520,7 @@
             jax.ShapeDtypeStruct((wid, rows), F32),
             jax.ShapeDtypeStruct((wid, rows), F32),
         ),
-        in_specs=[vmem, vmem, hbm, hbm],
+        in_specs=[hbm] * 4,
         out_specs=(vmem, vmem, vmem, vmem),
         scratch_shapes=[
             pltpu.VMEM((kc, ch), BF16),
@@ -469,19 +534,19 @@
             pltpu.VMEM((2, kc, half), BF16),
             pltpu.VMEM((2, kc, half), BF16),
             pltpu.VMEM((2, slots, longest, half), BF16),
-            pltpu.VMEM((2, half, rpad), BF16),
-            pltpu.VMEM((2, npx, wid, rpad), BF16),
-            dma((2,)),
+            [pltpu.VMEM((2, half, width), BF16) for width in widths],
+            [pltpu.VMEM((2, npx, wid, width), BF16) for width in widths],
+            dma((4,)),
             dma((4, 8)), dma((4, 8)),
             dma((2, 9)), dma((2, 9)),
             dma((2, slots, len(chunks))), dma((2, slots, len(chunks))),
             dma((2, half // wid, len(chunks))), dma((2, npx, len(chunks))),
         ],
         compiler_params=pltpu.CompilerParams(
-            collective_id=0, has_side_effects=True, vmem_limit_bytes=64000000
+            collective_id=0, has_side_effects=True, vmem_limit_bytes=48000000
         ),
         name="closure",
-    )(fields.reshape(block), cotangent.reshape(block), first_weight, second_weight)
+    )(*(pltpu.with_memory_space_constraint(v, pltpu.HBM) for v in (fields.reshape(block), cotangent.reshape(block), first_weight, second_weight)))
     out, fgrad, g1, g2 = pl.pallas_call(
         results,
         out_shape=(
@@ -490,9 +555,10 @@
             jax.ShapeDtypeStruct((wid, rows), F32),
             jax.ShapeDtypeStruct((wid, rows), F32),
         ),
-        in_specs=[hbm] * 4,
+        in_specs=[anywhere] * 4,
         out_specs=(hbm,) * 4,
         scratch_shapes=[dma((4,))],
+        compiler_params=pltpu.CompilerParams(vmem_limit_bytes=1 << 20),
         name="results",
     )(out, fgrad, g1, g2)
     return (

time: 119 us -> 62.5 us (0.53)
  Pallas kernels: 118 us -> 61.7 us
    pallas_call x1, Pallas kernels: 46.8 us -> 1.15 us  [body(): pl.pallas_call(results, out_shape=(jax.ShapeDtypeStruct(block, BF16), jax...]
    pallas_call x1, Pallas kernels: 71.6 us -> 60.6 us  [body(): pl.pallas_call(functools.partial(kernel, (ndp, npx, npy, batch * ndp)), o...]
where the time goes in v2:
time: 62.5 us; the launch traced here: 62.3 us
  Pallas kernels  61.7 us (99%)
  between operations  0.64 us (1%)
    pallas_call x1, Pallas kernels, body(): pl.pallas_call(functools.partial(kernel, (ndp, npx, npy, batch * ndp)), o...  60.6 us

profile of v2, /device:TPU:0, one launch (start us, length us, event | category | flops | bytes accessed | tf_op | source)
XLA Modules:
  0.0 62.3 jit_solution(11028121490024008974)
XLA Ops:
  0.6 60.6 %closure.1 = (bf16[4,8,32,256]{3,2,1,0:T(8,128)(2,1)S(1)}, bf16[4,8,32,256]{3,2,1,0:T(8,128)(2,1)S(1)}, f32[32,1728]{1,0:T(8,128)S(1)}, f32[32,1728]{1,0:T(8,128)S(1)}) custom-call(bf16[4,8,32,256]{3,2,1,0:T(8,128)(2,1)} %bitcast.6, bf16[4,8,32,256]{3,2,1,0:T(8,128)(2,1)} %bitcast.7, bf16[6912,256]{1,0:T(8,128)(2,1)} %w1_hbm.1, bf16[6912,256]{1,0:T(8,128)(2,1)} %w2_hbm.1), custom_call_target="tpu_custom_call" | custom-call | tf_op jit(solution)/shard_map/closure/pallas_call | solution.py:515
  61.2 1.1 %results.1 = (bf16[4,8,32,256]{3,2,1,0:T(8,128)(2,1)}, bf16[4,8,32,256]{3,2,1,0:T(8,128)(2,1)}, f32[32,1728]{1,0:T(8,128)}, f32[32,1728]{1,0:T(8,128)}) custom-call(bf16[4,8,32,256]{3,2,1,0:T(8,128)(2,1)S(1)} %get-tuple-element.12.refs_0_, bf16[4,8,32,256]{3,2,1,0:T(8,128)(2,1)S(1)} %get-tuple-element.13.refs_1_, f32[32,1728]{1,0:T(8,128)S(1)} %get-tuple-element.14.refs_2_, ...), custom_call_target="tpu_custom_call" | custom-call | tf_op jit(solution)/shard_map/results/pallas_call | solution.py:550

commit v3 on v2

--- a/solution.py
+++ b/solution.py
@@ -14,7 +14,8 @@
 ACROSS = [i for i, (dx, _) in enumerate(DIRS) if not dx]
 GELU_C = 0.7978845608028654
 GELU_A = 0.044715
-LAG = 2
+LAG = 1
+LOADS = 4
 
 
 def gelu_parts(v):
@@ -69,7 +70,7 @@
     out_ref, fgrad_ref, g1_ref, g2_ref,
     w1, w2, p_f, p_c, p_h, p_g, z_a, z_b, z_c, lhs_f, lhs_h, pre,
     own, send_a, recv_a, recv_b, send_z, recv_z,
-    sem_w, halo_send, halo_recv, a_send, a_recv, b_send, b_recv, z_send, z_recv,
+    sem_w, sem_f, halo_send, halo_recv, a_send, a_recv, b_send, b_recv, z_send, z_recv,
 ):
     ndp, npx, npy, rollouts = sizes
     nx, ny, nz, ch = fields.shape
@@ -83,14 +84,18 @@
     d, x, y = lax.axis_index("dp"), lax.axis_index("px"), lax.axis_index("py")
 
     inner = pl.ds(1, nx), pl.ds(1, ny)
-    load_f = pltpu.make_async_copy(fields, p_f.at[inner], sem_w.at[2])
-    load_c = pltpu.make_async_copy(cot, p_c.at[inner], sem_w.at[3])
-    load_w = [
-        pltpu.make_async_copy(w1_hbm, w1, sem_w.at[0]),
-        pltpu.make_async_copy(w2_hbm, w2, sem_w.at[1]),
-    ]
-    for copy in [load_f, load_c, *load_w]:
-        copy.start()
+    load_f = pltpu.make_async_copy(fields, p_f.at[inner], sem_f.at[0])
+    load_c = pltpu.make_async_copy(cot, p_c.at[inner], sem_f.at[1])
+    def load_w(which, action):
+        for n in range(LOADS):
+            part = pl.ds(n * (kc // LOADS), kc // LOADS)
+            source, target = ((w1_hbm, w1), (w2_hbm, w2))[which]
+            copy = pltpu.make_async_copy(source.at[part], target.at[part], sem_w.at[which, n])
+            copy.start() if action == "start" else copy.wait()
+
+    load_f.start()
+    load_w(0, "start")
+    load_c.start()
 
     barrier = pltpu.get_barrier_semaphore()
     for i in range(1, ndp):
@@ -168,12 +173,18 @@
 
     tile = ny * nz
 
-    def conv(shifted, weight, flipped, finish, *planes):
-        step = planes[1] - planes[0] if len(planes) > 1 else 1
-
-        @pl.loop(0, len(planes))
+    def conv(shifted, weight, flipped, finish, inside_first, beside, low=0, high=nx):
+        @pl.loop(low, high)
         def _(j):
-            i = planes[0] + j * step
+            for at, task in beside:
+                @pl.when(j == at)
+                def _():
+                    task()
+
+            if inside_first:
+                i = jnp.where(j < nx - 2, j + 1, (j - (nx - 2)) * (nx - 1))
+            else:
+                i = jnp.where(j < 2, j * (nx - 1), j - 1)
             total = None
             for a in range(3):
                 for b in range(3):
@@ -198,7 +209,6 @@
                         total = term if total is None else total + term
             finish(i, total)
 
-    edges, middle = sorted({0, nx - 1}), range(1, nx - 1)
     partner = 1 - y
 
     def a_copy(which, step):
@@ -277,36 +287,44 @@
                     if (hb if chunks[chunk][0] == 0 else ha) > 0:
                         b_copy(which, 0, ha, hb, chunk).start()
 
+    after = [-(-(count + LAG) // 3) for count in done]
+
     def weight_grad(which, lhs, shifted, beside):
-        def one(t, left):
+        def three(group, left):
+            for k in range(len(hops)):
+                if after[k] < 3:
+                    @pl.when(group == after[k])
+                    def _():
+                        piece_start(which, k)
+
             for at, task in beside:
-                @pl.when(t == at)
+                @pl.when(group == at)
                 def _():
                     task()
 
-            for k in range(len(hops)):
-                if done[k] + LAG < 9:
-                    @pl.when(t == done[k] + LAG)
-                    def _():
-                        piece_start(which, k)
-            step = lax.rem(left, 9)
-            a, b = step // 3, lax.rem(step, 3)
-            rhs = shifted[pl.ds(2 - a, nx), pl.ds(2 - b, ny)].reshape(cells, 3 * ch)
-            prod = jnp.dot(lhs[...], rhs, preferred_element_type=F32)
-            for c in range(3):
-                block = prod[:, (2 - c) * ch : (3 - c) * ch]
-                here = pl.ds(pl.multiple_of(step * 3 * ch, ch) + c * ch, ch)
-                low, high = block[:, :half], block[:, half:]
-                own[which, here] = jnp.where(y == 0, low, high)
-                send_a[which, here] = jnp.where(y == 0, high, low).astype(BF16)
-            a_copy(which, step).start()
-            return left // 9
-
-        lax.fori_loop(0, 9, one, code)
+            steps = []
+            for _ in range(3):
+                step = lax.rem(left, 9)
+                steps.append(step)
+                left = left // 9
+                a, b = step // 3, lax.rem(step, 3)
+                rhs = shifted[pl.ds(2 - a, nx), pl.ds(2 - b, ny)].reshape(cells, 3 * ch)
+                prod = jnp.dot(lhs[...], rhs, preferred_element_type=F32)
+                for c in range(3):
+                    block = prod[:, (2 - c) * ch : (3 - c) * ch]
+                    here = pl.ds(pl.multiple_of(step * 3 * ch, ch) + c * ch, ch)
+                    low, high = block[:, :half], block[:, half:]
+                    own[which, here] = jnp.where(y == 0, low, high)
+                    send_a[which, here] = jnp.where(y == 0, high, low).astype(BF16)
+            for step in steps:
+                a_copy(which, step).start()
+            return left
+
+        lax.fori_loop(0, 3, three, code)
 
     def pieces_rest(which):
         for k in range(len(hops)):
-            if done[k] + LAG >= 9 and k < len(hops) - 1:
+            if after[k] >= 3 and k < len(hops) - 1:
                 piece_start(which, k)
 
     def own_piece(which):
@@ -403,8 +421,8 @@
     every = range(len(chunks))
 
     load_f.wait()
+    halo_start(0, p_f, 1, p_f, ACROSS)
     halo_start(0, p_f, 1, p_f, ALONG)
-    halo_start(0, p_f, 1, p_f, ACROSS)
     load_c.wait()
     halo_start(1, p_c, 1, p_c, ACROSS)
     halo_wait(0, p_f, 1, p_f, ACROSS)
@@ -415,24 +433,21 @@
         value = (total * (0.5 * (1.0 + gelu_parts(total)))).astype(BF16)
         p_h[i + 1, pl.ds(1, ny)] = value.reshape(ny, nz, ch)
 
-    load_w[0].wait()
-    conv(z_a, w1, False, hidden_finish, *middle)
-    halo_start(1, p_c, 1, p_c, ALONG)
-    halo_wait(1, p_c, 1, p_c, ACROSS)
-    build(p_c, z_b, 1, nx + 1)
-    halo_wait(0, p_f, 1, p_f, ALONG)
-    build(p_f, z_a, 0, 2, nx + 1)
-    conv(z_a, w1, False, hidden_finish, *edges)
+    load_w(0, "wait")
+    load_w(1, "start")
+    def outer_fields():
+        halo_start(1, p_c, 1, p_c, ALONG)
+        halo_wait(1, p_c, 1, p_c, ACROSS)
+        build(p_c, z_b, 1, nx + 1)
+        halo_wait(0, p_f, 1, p_f, ALONG)
+        build(p_f, z_a, 0, 2, nx + 1)
+
+    conv(z_a, w1, False, hidden_finish, True, [(nx - 2, outer_fields)])
     halo_start(2, p_h, 1, p_h, ALONG)
     halo_start(2, p_h, 1, p_h, ACROSS)
     lhs_h[...] = p_h[pl.ds(1, nx), pl.ds(1, ny)].reshape(cells, ch).T
     halo_wait(1, p_c, 1, p_c, ALONG)
     build(p_c, z_b, 0, 2, nx + 1)
-    weight_grad(1, lhs_h, z_b, [])
-    pieces_rest(1)
-    advance(1, 0)
-    load_w[1].wait()
-
     def grad_finish(i, total):
         v = pre[i]
         t = gelu_parts(v)
@@ -441,48 +456,60 @@
         )
         p_g[i + 1, pl.ds(1, ny)] = (total * slope).astype(BF16).reshape(ny, nz, ch)
 
-    conv(z_b, w2, True, grad_finish, *edges)
-    halo_start(3, p_g, 1, p_g, ALONG)
+    def outer_grad():
+        load_w(1, "wait")
+        conv(z_b, w2, True, grad_finish, False, [], 0, 2)
+        halo_start(3, p_g, 1, p_g, ALONG)
+
+    weight_grad(1, lhs_h, z_b, [(2, outer_grad)])
+    pieces_rest(1)
+    advance(1, 0)
+    conv(z_b, w2, True, grad_finish, False, [], 2, nx)
+    halo_start(3, p_g, 1, p_g, ACROSS)
     own_piece(1)
     advance(1, 1)
-    conv(z_b, w2, True, grad_finish, *middle)
-    halo_start(3, p_g, 1, p_g, ACROSS)
     lhs_f[...] = p_f[inner].reshape(cells, ch).T
     halo_wait(2, p_h, 1, p_h, ALONG)
     halo_wait(2, p_h, 1, p_h, ACROSS)
     build(p_h, z_a, 0, nx + 2)
-    columns_send(1, 0)
-
-    def out_finish(i, total):
-        out_ref[i] = (
-            (p_f[i + 1, pl.ds(1, ny)].reshape(tile, ch).astype(F32) + total).astype(BF16).reshape(ny, nz, ch)
-        )
-
-    conv(z_a, w2, False, out_finish, *range(nx // 2))
-    advance(1, 2)
     halo_wait(3, p_g, 1, p_g, ACROSS)
     build(p_g, z_c, 1, nx + 1)
     halo_wait(3, p_g, 1, p_g, ALONG)
     build(p_g, z_c, 0, 2, nx + 1)
     weight_grad(
         0, lhs_f, z_c,
-        [(1, lambda: columns_send(1, 1)), (7, lambda: columns_send(1, 2))],
+        [
+            (0, lambda: columns_send(1, 0)),
+            (1, lambda: advance(1, 2)),
+            (2, lambda: columns_send(1, 1)),
+        ],
     )
     pieces_rest(0)
-    advance(0, 0)
-    conv(z_a, w2, False, out_finish, *range(nx // 2, nx))
-    own_piece(0)
-    advance(0, 1)
+
+    def out_finish(i, total):
+        out_ref[i] = (
+            (p_f[i + 1, pl.ds(1, ny)].reshape(tile, ch).astype(F32) + total)
+            .astype(BF16)
+            .reshape(ny, nz, ch)
+        )
+
+    def own_next():
+        own_piece(0)
+        advance(0, 1)
+
+    conv(z_a, w2, False, out_finish, True, [(1, lambda: advance(0, 0)), (2, own_next), (3, lambda: columns_send(1, 2))])
 
     def field_finish(i, total):
         fgrad_ref[i] = (
-            (p_c[i + 1, pl.ds(1, ny)].reshape(tile, ch).astype(F32) + total).astype(BF16).reshape(ny, nz, ch)
-        )
-
-    conv(z_c, w1, True, field_finish, *edges)
-    columns_send(0, 0)
-    advance(0, 2)
-    conv(z_c, w1, True, field_finish, *middle)
+            (p_c[i + 1, pl.ds(1, ny)].reshape(tile, ch).astype(F32) + total)
+            .astype(BF16)
+            .reshape(ny, nz, ch)
+        )
+
+    conv(
+        z_c, w1, True, field_finish, True,
+        [(1, lambda: columns_send(0, 0)), (3, lambda: advance(0, 2))],
+    )
     for chunk in every:
         finish_grad(1, g2_ref, chunk)
     sent(1)
@@ -536,7 +563,7 @@
             pltpu.VMEM((2, slots, longest, half), BF16),
             [pltpu.VMEM((2, half, width), BF16) for width in widths],
             [pltpu.VMEM((2, npx, wid, width), BF16) for width in widths],
-            dma((4,)),
+            dma((2, LOADS)), dma((2,)),
             dma((4, 8)), dma((4, 8)),
             dma((2, 9)), dma((2, 9)),
             dma((2, slots, len(chunks))), dma((2, slots, len(chunks))),

time: 62.5 us -> 61.1 us (0.978)
  Pallas kernels: 61.7 us -> 60.3 us
    pallas_call x1, Pallas kernels: 60.6 us -> 59.2 us  [body(): pl.pallas_call(functools.partial(kernel, (ndp, npx, npy, batch * ndp)), o...]
where the time goes in v3:
time: 61.1 us; the launch traced here: 61 us
  Pallas kernels  60.3 us (99%)
  between operations  0.64 us (1%)
    pallas_call x1, Pallas kernels, body(): pl.pallas_call(functools.partial(kernel, (ndp, npx, npy, batch * ndp)), o...  59.2 us

profile of v3, /device:TPU:0, one launch (start us, length us, event | category | flops | bytes accessed | tf_op | source)
XLA Modules:
  0.0 61.0 jit_solution(8812317117940953295)
XLA Ops:
  0.6 59.2 %closure.1 = (bf16[4,8,32,256]{3,2,1,0:T(8,128)(2,1)S(1)}, bf16[4,8,32,256]{3,2,1,0:T(8,128)(2,1)S(1)}, f32[32,1728]{1,0:T(8,128)S(1)}, f32[32,1728]{1,0:T(8,128)S(1)}) custom-call(bf16[4,8,32,256]{3,2,1,0:T(8,128)(2,1)} %bitcast.6, bf16[4,8,32,256]{3,2,1,0:T(8,128)(2,1)} %bitcast.7, bf16[6912,256]{1,0:T(8,128)(2,1)} %w1_hbm.1, bf16[6912,256]{1,0:T(8,128)(2,1)} %w2_hbm.1), custom_call_target="tpu_custom_call" | custom-call | tf_op jit(solution)/shard_map/closure/pallas_call | solution.py:542
  59.8 1.1 %results.1 = (bf16[4,8,32,256]{3,2,1,0:T(8,128)(2,1)}, bf16[4,8,32,256]{3,2,1,0:T(8,128)(2,1)}, f32[32,1728]{1,0:T(8,128)}, f32[32,1728]{1,0:T(8,128)}) custom-call(bf16[4,8,32,256]{3,2,1,0:T(8,128)(2,1)S(1)} %get-tuple-element.12.refs_0_, bf16[4,8,32,256]{3,2,1,0:T(8,128)(2,1)S(1)} %get-tuple-element.13.refs_1_, f32[32,1728]{1,0:T(8,128)S(1)} %get-tuple-element.14.refs_2_, ...), custom_call_target="tpu_custom_call" | custom-call | tf_op jit(solution)/shard_map/results/pallas_call | solution.py:577

commit v4 on v3

--- a/solution.py
+++ b/solution.py
@@ -44,8 +44,9 @@
     for side, (low, high) in enumerate(((0, first), (first, rows))):
         tiles, start = -(-(high - low) // 128), low
         for left in range(min(3, tiles), 0, -1):
-            stop = min(high, start + -(-tiles // left) * 128)
-            tiles -= -(-tiles // left)
+            take = tiles if left == 1 else max(1, min(-(-tiles // 2), tiles - left + 1, 3))
+            stop = min(high, start + take * 128)
+            tiles -= take
             chunks.append((side, start, start - low, stop - start))
             start = stop
     return (da, db), hops, codes, done, chunks

time: 61.1 us -> 61.1 us (level)
  no operation moved by 1% of the time
where the time goes in v4:
time: 61.1 us; the launch traced here: 61 us
  Pallas kernels  60.3 us (99%)
  between operations  0.64 us (1%)
    pallas_call x1, Pallas kernels, body(): pl.pallas_call(functools.partial(kernel, (ndp, npx, npy, batch * ndp)), o...  59.2 us

profile of v4, /device:TPU:0, one launch (start us, length us, event | category | flops | bytes accessed | tf_op | source)
XLA Modules:
  0.0 61.0 jit_solution(8812317117940953295)
XLA Ops:
  0.6 59.2 %closure.1 = (bf16[4,8,32,256]{3,2,1,0:T(8,128)(2,1)S(1)}, bf16[4,8,32,256]{3,2,1,0:T(8,128)(2,1)S(1)}, f32[32,1728]{1,0:T(8,128)S(1)}, f32[32,1728]{1,0:T(8,128)S(1)}) custom-call(bf16[4,8,32,256]{3,2,1,0:T(8,128)(2,1)} %bitcast.6, bf16[4,8,32,256]{3,2,1,0:T(8,128)(2,1)} %bitcast.7, bf16[6912,256]{1,0:T(8,128)(2,1)} %w1_hbm.1, bf16[6912,256]{1,0:T(8,128)(2,1)} %w2_hbm.1), custom_call_target="tpu_custom_call" | custom-call | tf_op jit(solution)/shard_map/closure/pallas_call | solution.py:543
  59.8 1.1 %results.1 = (bf16[4,8,32,256]{3,2,1,0:T(8,128)(2,1)}, bf16[4,8,32,256]{3,2,1,0:T(8,128)(2,1)}, f32[32,1728]{1,0:T(8,128)}, f32[32,1728]{1,0:T(8,128)}) custom-call(bf16[4,8,32,256]{3,2,1,0:T(8,128)(2,1)S(1)} %get-tuple-element.12.refs_0_, bf16[4,8,32,256]{3,2,1,0:T(8,128)(2,1)S(1)} %get-tuple-element.13.refs_1_, f32[32,1728]{1,0:T(8,128)S(1)} %get-tuple-element.14.refs_2_, ...), custom_call_target="tpu_custom_call" | custom-call | tf_op jit(solution)/shard_map/results/pallas_call | solution.py:578
